TPU v7x, 32 devices: a whole 2x2x4 slice. The times are simulated.
32 devices in a mesh: dp: 4 (over z), row: 2 (over x), col: 4 (over y, core).
Axes of the slice: x: 2, y: 2, z: 4, core: 2. Of those that a mesh axis runs over, the one named last changes fastest.
Arguments:
- inputs: bfloat16 [4096, 1024], P(('dp', 'col'), 'row'), may hold values from -12 to 12
- qkv_weight: bfloat16 [1024, 3, 1024], P('row', None, 'col'), may hold values from -10 to 10
- qv_bias: float32 [2, 1024], P(None, 'col'), may hold values from -3 to 3
- out_weight: bfloat16 [1024, 1024], P('col', 'row'), may hold values from -1 to 1
- out_bias: float32 [1024], P('row'), may hold values from -3 to 3
- first_gain: float32 [1024], P('row'), may hold values from 0.1 to 1.9
- first_shift: float32 [1024], P('row'), may hold values from -3 to 3
- up_weight: bfloat16 [1024, 4096], P('row', 'col'), may hold values from -0.1875 to 0.1875
- up_bias: float32 [4096], P('col'), may hold values from -3 to 3
- down_weight: bfloat16 [4096, 1024], P('col', 'row'), may hold values from -0.09375 to 0.09375
- down_bias: float32 [1024], P('row'), may hold values from -3 to 3
- second_gain: float32 [1024], P('row'), may hold values from 0.1 to 1.9
- second_shift: float32 [1024], P('row'), may hold values from -3 to 3
- lengths: int32 [8], P(('dp', 'row')), may hold values from 128 to 512, as said below
- out_grad: bfloat16 [4096, 1024], P(('dp', 'col'), 'row'), may hold values from -9 to 9
Outputs:
- block_out: bfloat16 [4096, 1024], P(('dp', 'col'), 'row')
- grad_inputs: float32 [4096, 1024], P(('dp', 'col'), 'row')
- grad_qkv_weight: float32 [1024, 3, 1024], P('row', None, 'col')
- grad_qv_bias: float32 [2, 1024], P(None, 'col')
- grad_out_weight: float32 [1024, 1024], P('col', 'row')
- grad_out_bias: float32 [1024], P('row')
- grad_first_gain: float32 [1024], P('row')
- grad_first_shift: float32 [1024], P('row')
- grad_up_weight: float32 [1024, 4096], P('row', 'col')
- grad_up_bias: float32 [4096], P('col')
- grad_down_weight: float32 [4096, 1024], P('col', 'row')
- grad_down_bias: float32 [1024], P('row')
- grad_second_gain: float32 [1024], P('row')
- grad_second_shift: float32 [1024], P('row')
Inputs may be any that keep to these rules, and one draw needn't show every extreme that they name: `lengths`: positions at or past a sequence's length are padding.
All inputs are finite; a program needn't handle non-finite values.
Results may differ from a plain program's by a relative error of at most 0.013.
The roundings to bfloat16 on the way count: a program that leaves them out, or rounds other values in their place, can miss the bound.
Values may be sent and summed in bfloat16 or wider, within the bound.
A program may use at most 128 MiB of HBM per device.

v0:
```python
import jax
import jax.numpy as jnp
from jax import lax
from jax.sharding import PartitionSpec as P

MODEL_WIDTH = 1024
HEADS = 16
HEAD_DIM = 64
L = 512


norm_epsilon = 1e-12
masked_score = -1e30
root_half = 0.7071067811865476
gauss_height = 0.3989422804014327


def forward_gather(block):
    return lax.all_gather(block, "col", axis=0, tiled=True)


def forward_reduce(product_term, row_count):
    return lax.psum_scatter(
        product_term(jnp.int32(0), row_count * lax.axis_size("row")),
        "row",
        scatter_dimension=0,
        tiled=True,
    )


def forward_collect(block):
    return lax.all_gather(block, "row", axis=0, tiled=True)


def forward_combine(product_term, row_count):
    return lax.psum_scatter(
        product_term(jnp.int32(0), row_count * lax.axis_size("col")),
        "col",
        scatter_dimension=0,
        tiled=True,
    )


def backward_gather(block):
    return lax.all_gather(block, "col", axis=0, tiled=True)


def backward_reduce(product_term, row_count):
    return lax.psum_scatter(
        product_term(jnp.int32(0), row_count * lax.axis_size("row")),
        "row",
        scatter_dimension=0,
        tiled=True,
    )


def backward_collect(block):
    return lax.all_gather(block, "row", axis=0, tiled=True)


def backward_combine(product_term, row_count):
    return lax.psum_scatter(
        product_term(jnp.int32(0), row_count * lax.axis_size("col")),
        "col",
        scatter_dimension=0,
        tiled=True,
    )


def width_pair(first_part, second_part):
    return lax.psum((first_part, second_part), "row")


def rows_times(gathered, weight):

    def product_term(first_row, row_count):
        return jnp.dot(gathered, weight, preferred_element_type=jnp.float32)

    return product_term


def rows_times_turned(gathered, weight):

    def product_term(first_row, row_count):
        return lax.dot_general(
            gathered, weight, (((1,), (1,)), ((), ())), preferred_element_type=jnp.float32
        )

    return product_term


def contract_rows(first_side, second_side):
    return lax.dot_general(
        first_side, second_side, (((0,), (0,)), ((), ())), preferred_element_type=jnp.float32
    )


def gelu_pair(preact):
    lower_mass = 0.5 * (1.0 + lax.erf(preact * root_half))
    return (
        preact * lower_mass,
        lower_mass + preact * jnp.exp(-0.5 * preact * preact) * gauss_height,
    )


def norm_forward(hidden, norm_gain, norm_shift):
    center, square = width_pair(
        jnp.sum(hidden, axis=-1, keepdims=True), jnp.sum(hidden * hidden, axis=-1, keepdims=True)
    )
    center = center / MODEL_WIDTH
    square = square / MODEL_WIDTH
    rscale = lax.rsqrt(square - center * center + norm_epsilon)
    normed = (hidden - center) * rscale
    return (normed * norm_gain + norm_shift, normed, rscale)


def norm_back(incoming_gradient, normed, rscale, norm_gain):
    scaled = incoming_gradient * norm_gain
    first_mean, second_mean = width_pair(
        jnp.sum(scaled, axis=-1, keepdims=True), jnp.sum(scaled * normed, axis=-1, keepdims=True)
    )
    return rscale * (scaled - first_mean / MODEL_WIDTH - normed * (second_mean / MODEL_WIDTH))


def score_block(queries, keys_low, lengths):
    scores = jnp.einsum(
        "sqhd,skhd->shqk", queries, keys_low, preferred_element_type=jnp.float32
    ) * HEAD_DIM ** (-0.5)
    visible = lax.broadcasted_iota(jnp.int32, (1, 1, 1, L), 3) < lengths[:, None, None, None]
    return jnp.where(visible, scores, masked_score)


def attend(queries, keys_low, values, lengths):
    scores = score_block(queries, keys_low, lengths)
    row_peak = jnp.max(scores, axis=3, keepdims=True)
    logsum = row_peak + jnp.log(jnp.sum(jnp.exp(scores - row_peak), axis=3, keepdims=True))
    soft_weights = jnp.exp(scores - logsum).astype(jnp.bfloat16)
    attention_output = jnp.einsum(
        "shqk,skhd->sqhd", soft_weights, values, preferred_element_type=jnp.float32
    )
    return (attention_output.astype(jnp.bfloat16), logsum)


def attend_back(queries, keys_low, values, logsum, incoming_gradient, lengths):
    scores = score_block(queries, keys_low, lengths)
    soft_weights = jnp.exp(scores - logsum)
    grad_weights = jnp.einsum(
        "sqhd,skhd->shqk", incoming_gradient, values, preferred_element_type=jnp.float32
    )
    row_inner = jnp.sum(soft_weights * grad_weights, axis=3, keepdims=True)
    score_grad = (soft_weights * (grad_weights - row_inner)).astype(jnp.bfloat16)
    score_scale = HEAD_DIM ** (-0.5)
    grad_queries = (
        jnp.einsum("shqk,skhd->sqhd", score_grad, keys_low, preferred_element_type=jnp.float32)
        * score_scale
    )
    grad_keys = (
        jnp.einsum("shqk,sqhd->skhd", score_grad, queries, preferred_element_type=jnp.float32)
        * score_scale
    )
    grad_values = jnp.einsum(
        "shqk,sqhd->skhd",
        soft_weights.astype(jnp.bfloat16),
        incoming_gradient,
        preferred_element_type=jnp.float32,
    )
    return (grad_queries, grad_keys, grad_values)


def shards(
    inputs,
    qkv_weight,
    qv_bias,
    out_weight,
    out_bias,
    first_gain,
    first_shift,
    up_weight,
    up_bias,
    down_weight,
    down_bias,
    second_gain,
    second_shift,
    lengths,
    out_grad,
):
    head_local = HEADS // lax.axis_size("col")
    seq_local = lengths.shape[0]
    head_shape = (seq_local, L, head_local, HEAD_DIM)
    qkv_flat = qkv_weight.reshape(qkv_weight.shape[0], -1)
    across_rows = inputs.shape[0]
    gathered_in = forward_gather(inputs)
    down_rows = gathered_in.shape[0] // lax.axis_size("row")
    projected = forward_reduce(rows_times(gathered_in, qkv_flat), down_rows).reshape(
        down_rows, 3, -1
    )
    queries = (projected[:, 0] + qv_bias[0]).astype(jnp.bfloat16).reshape(head_shape)
    keys_low = projected[:, 1].astype(jnp.bfloat16).reshape(head_shape)
    values = (projected[:, 2] + qv_bias[1]).astype(jnp.bfloat16).reshape(head_shape)
    attention_output, logsum = attend(queries, keys_low, values, lengths)
    gathered_att = forward_collect(attention_output.reshape(down_rows, -1))
    first_sum = (
        inputs.astype(jnp.float32)
        + forward_combine(rows_times(gathered_att, out_weight), across_rows)
        + out_bias
    )
    first_norm, first_standardized, first_scale = norm_forward(first_sum, first_gain, first_shift)
    gathered_norm = forward_gather(first_norm.astype(jnp.bfloat16))
    preact = forward_reduce(rows_times(gathered_norm, up_weight), down_rows) + up_bias
    activated, gelu_slope = gelu_pair(preact)
    gathered_act = forward_collect(activated.astype(jnp.bfloat16))
    second_sum = (
        first_norm + forward_combine(rows_times(gathered_act, down_weight), across_rows) + down_bias
    )
    second_norm, second_standardized, second_scale = norm_forward(
        second_sum, second_gain, second_shift
    )
    block_out = second_norm.astype(jnp.bfloat16)
    incoming_gradient = out_grad.astype(jnp.float32)
    second_norm_gradient = norm_back(
        incoming_gradient, second_standardized, second_scale, second_gain
    )
    gathered_grad = backward_gather(second_norm_gradient.astype(jnp.bfloat16))
    grad_down = contract_rows(gathered_act, gathered_grad)
    preactivation_gradient = (
        backward_reduce(rows_times_turned(gathered_grad, down_weight), down_rows) * gelu_slope
    )
    gathered_pre = backward_collect(preactivation_gradient.astype(jnp.bfloat16))
    grad_up = contract_rows(gathered_norm, gathered_pre)
    norm_gradient_total = second_norm_gradient + backward_combine(
        rows_times_turned(gathered_pre, up_weight), across_rows
    )
    first_norm_gradient = norm_back(
        norm_gradient_total, first_standardized, first_scale, first_gain
    )
    gathered_first = backward_gather(first_norm_gradient.astype(jnp.bfloat16))
    grad_out = contract_rows(gathered_att, gathered_first)
    attended_grad = (
        backward_reduce(rows_times_turned(gathered_first, out_weight), down_rows)
        .astype(jnp.bfloat16)
        .reshape(head_shape)
    )
    grad_queries, grad_keys, grad_values = attend_back(
        queries, keys_low, values, logsum, attended_grad, lengths
    )
    query_rows_flattened = grad_queries.reshape(down_rows, -1)
    value_rows_flattened = grad_values.reshape(down_rows, -1)
    combined_heads = (
        jnp.stack(
            [query_rows_flattened, grad_keys.reshape(down_rows, -1), value_rows_flattened], axis=1
        )
        .astype(jnp.bfloat16)
        .reshape(down_rows, -1)
    )
    gathered_joined = backward_collect(combined_heads)
    grad_qkv = contract_rows(gathered_in, gathered_joined).reshape(qkv_weight.shape)
    grad_inputs = first_norm_gradient + backward_combine(
        rows_times_turned(gathered_joined, qkv_flat), across_rows
    )
    column_sums = lax.psum(
        (
            jnp.sum(first_norm_gradient, axis=0),
            jnp.sum(norm_gradient_total * first_standardized, axis=0),
            jnp.sum(norm_gradient_total, axis=0),
            jnp.sum(second_norm_gradient, axis=0),
            jnp.sum(incoming_gradient * second_standardized, axis=0),
            jnp.sum(incoming_gradient, axis=0),
        ),
        ("dp", "col"),
    )
    row_sums = lax.psum(
        (
            jnp.stack(
                [jnp.sum(query_rows_flattened, axis=0), jnp.sum(value_rows_flattened, axis=0)]
            ),
            jnp.sum(preactivation_gradient, axis=0),
        ),
        ("dp", "row"),
    )
    grad_qkv, grad_out, grad_up, grad_down = (
        lax.psum(grad_qkv.astype(jnp.bfloat16), "dp").astype(jnp.float32),
        lax.psum(grad_out.astype(jnp.bfloat16), "dp").astype(jnp.float32),
        lax.psum(grad_up.astype(jnp.bfloat16), "dp").astype(jnp.float32),
        lax.psum(grad_down.astype(jnp.bfloat16), "dp").astype(jnp.float32),
    )
    return (
        block_out,
        grad_inputs,
        grad_qkv,
        row_sums[0],
        grad_out,
        column_sums[0],
        column_sums[1],
        column_sums[2],
        grad_up,
        row_sums[1],
        grad_down,
        column_sums[3],
        column_sums[4],
        column_sums[5],
    )


def solution(mesh):
    in_specs = (
        P(("dp", "col"), "row"),
        P("row", None, "col"),
        P(None, "col"),
        P("col", "row"),
        P("row"),
        P("row"),
        P("row"),
        P("row", "col"),
        P("col"),
        P("col", "row"),
        P("row"),
        P("row"),
        P("row"),
        P(("dp", "row")),
        P(("dp", "col"), "row"),
    )
    out_specs = (
        P(("dp", "col"), "row"),
        P(("dp", "col"), "row"),
        P("row", None, "col"),
        P(None, "col"),
        P("col", "row"),
        P("row"),
        P("row"),
        P("row"),
        P("row", "col"),
        P("col"),
        P("col", "row"),
        P("row"),
        P("row"),
        P("row"),
    )
    return jax.shard_map(shards, mesh=mesh, in_specs=in_specs, out_specs=out_specs, check_vma=False)
```

profile of v0, /device:TPU:0, one launch (start us, length us, event | category | flops | bytes accessed | tf_op | source)
XLA Modules:
  0.0 701.3 jit_solution(1587023572651374637)
XLA Ops:
  9.4 19.6 %all-gather.8.cloned.1.call-done = bf16[1024,512]{1,0:T(8,128)(2,1)} async-done(((bf16[256,512]{1,0:T(8,128)(2,1)}), bf16[1024,512]{1,0:T(8,128)(2,1)}) %all-gather.8.cloned.1.call-update) | async-done | bytes 1048592 | tf_op jit(solution)/shard_map/all_gather | solution.py:19
  33.9 42.7 %reduce-scatter.9.cloned.1.call-done = f32[512,768]{1,0:T(8,128)} async-done(((f32[1024,768]{1,0:T(8,128)}), f32[512,768]{1,0:T(8,128)}) %reduce-scatter.9.cloned.1.call-update) | async-done | bytes 1572880 | tf_op jit(solution)/shard_map/reduce_scatter | solution.py:23
  83.1 8.5 %all_gather.25 = bf16[1024,256]{0,1:T(8,128)(2,1)S(1)} all-gather(bf16[512,256]{0,1:T(8,128)(2,1)S(1)} %bitcast.93), channel_id=1, replica_groups=mesh['dp'=4,'row'=2,'col'=4] {'row'}, dimensions={0}, use_global_device_ids=true | all-gather | bytes 786432 | tf_op jit(solution)/shard_map/all_gather | solution.py:32
  94.3 31.3 %reduce-scatter.11.cloned.1.call-done = f32[256,512]{1,0:T(8,128)} async-done(((f32[1024,512]{1,0:T(8,128)}), f32[256,512]{1,0:T(8,128)}) %reduce-scatter.11.cloned.1.call-update) | async-done | bytes 524304 | tf_op jit(solution)/shard_map/reduce_scatter | solution.py:36
  127.6 4.9 all-reduce.5
  134.5 16.8 %all-gather.10.cloned.1.call-done = bf16[1024,512]{1,0:T(8,128)(2,1)} async-done(((bf16[256,512]{1,0:T(8,128)(2,1)}), bf16[1024,512]{1,0:T(8,128)(2,1)}) %all-gather.10.cloned.1.call-update) | async-done | bytes 1048592 | tf_op jit(solution)/shard_map/all_gather | solution.py:19
  151.3 4.8 fusion.31
  156.1 54.5 %reduce-scatter.13.cloned.1.call-done = f32[512,1024]{1,0:T(8,128)} async-done(((f32[1024,1024]{1,0:T(8,128)}), f32[512,1024]{1,0:T(8,128)}) %reduce-scatter.13.cloned.1.call-update) | async-done | bytes 2097168 | tf_op jit(solution)/shard_map/reduce_scatter | solution.py:23
  213.7 33.2 %all-gather.12.cloned.1.call-done = bf16[1024,1024]{1,0:T(8,128)(2,1)} async-done(((bf16[512,1024]{1,0:T(8,128)(2,1)}), bf16[1024,1024]{1,0:T(8,128)(2,1)}) %all-gather.12.cloned.1.call-update) | async-done | bytes 2097168 | tf_op jit(solution)/shard_map/all_gather | solution.py:32
  251.1 31.3 %reduce-scatter.15.cloned.1.call-done = f32[256,512]{1,0:T(8,128)} async-done(((f32[1024,512]{1,0:T(8,128)}), f32[256,512]{1,0:T(8,128)}) %reduce-scatter.15.cloned.1.call-update) | async-done | bytes 524304 | tf_op jit(solution)/shard_map/reduce_scatter | solution.py:36
  284.6 4.9 all-reduce.4
  291.0 4.9 all-reduce.3
  299.6 16.8 %all-gather.14.cloned.1.call-done = bf16[1024,512]{1,0:T(8,128)(2,1)} async-done(((bf16[256,512]{1,0:T(8,128)(2,1)}), bf16[1024,512]{1,0:T(8,128)(2,1)}) %all-gather.14.cloned.1.call-update) | async-done | bytes 1048592 | tf_op jit(solution)/shard_map/all_gather | solution.py:45
  321.0 54.5 %reduce-scatter.17.cloned.1.call-done = f32[512,1024]{1,0:T(8,128)} async-done(((f32[1024,1024]{1,0:T(8,128)}), f32[512,1024]{1,0:T(8,128)}) %reduce-scatter.17.cloned.1.call-update) | async-done | bytes 2097168 | tf_op jit(solution)/shard_map/reduce_scatter | solution.py:49
  379.2 33.0 %all-gather.16.cloned.1.call-done = bf16[1024,1024]{1,0:T(8,128)(2,1)} async-done(((bf16[512,1024]{1,0:T(8,128)(2,1)}), bf16[1024,1024]{1,0:T(8,128)(2,1)}) %all-gather.16.cloned.1.call-update) | async-done | bytes 2097168 | tf_op jit(solution)/shard_map/all_gather | solution.py:58
  416.5 31.3 %reduce-scatter.19.cloned.1.call-done = f32[256,512]{1,0:T(8,128)} async-done(((f32[1024,512]{1,0:T(8,128)}), f32[256,512]{1,0:T(8,128)}) %reduce-scatter.19.cloned.1.call-update) | async-done | bytes 524304 | tf_op jit(solution)/shard_map/reduce_scatter | solution.py:62
  449.8 4.9 all-reduce.2
  456.9 16.8 %all-gather.18.cloned.1.call-done = bf16[1024,512]{1,0:T(8,128)(2,1)} async-done(((bf16[256,512]{1,0:T(8,128)(2,1)}), bf16[1024,512]{1,0:T(8,128)(2,1)}) %all-gather.18.cloned.1.call-update) | async-done | bytes 1048592 | tf_op jit(solution)/shard_map/all_gather | solution.py:45
  476.5 20.5 %reduce-scatter.21.cloned.1.call-done = f32[512,256]{1,0:T(8,128)} async-done(((f32[1024,256]{1,0:T(8,128)}), f32[512,256]{1,0:T(8,128)}) %reduce-scatter.21.cloned.1.call-update) | async-done | bytes 524304 | tf_op jit(solution)/shard_map/reduce_scatter | solution.py:49
  514.9 19.4 %all-gather.20.cloned.1.call-done = bf16[1024,768]{0,1:T(8,128)(2,1)} async-done(((bf16[512,768]{0,1:T(8,128)(2,1)}), bf16[1024,768]{0,1:T(8,128)(2,1)}) %all-gather.20.cloned.1.call-update) | async-done | bytes 1572880 | tf_op jit(solution)/shard_map/all_gather | solution.py:58
  541.1 65.0 %all-reduce = (f32[512]{0:T(512)}, f32[512]{0:T(512)}, f32[512]{0:T(512)}, f32[512]{0:T(512)}, f32[512]{0:T(512)}, /*index=5*/f32[512]{0:T(512)}) all-reduce(f32[512]{0:T(512)S(1)} %get-tuple-element.50, f32[512]{0:T(512)S(1)} %get-tuple-element.14, ...), channel_id=1, replica_groups=mesh['dp'=4,'row'=2,'col'=4] {'dp','col'}, use_global_device_ids=true, to_apply=%region_33.34 | all-reduce | flops 3072 | bytes 24576 | tf_op jit(solution)/shard_map/psum | solution.py:260
  606.2 19.9 %all-reduce.1 = (f32[2,256]{1,0:T(2,128)}, f32[1024]{0:T(1024)}) all-reduce(f32[2,256]{1,0:T(2,128)S(1)} %pad_maximum_fusion.1, f32[1024]{0:T(1024)S(1)} %get-tuple-element.52), channel_id=1, replica_groups=mesh['dp'=4,'row'=2,'col'=4] {'dp','row'}, use_global_device_ids=true, to_apply=%region_30.31 | all-reduce | flops 1536 | bytes 12288 | tf_op jit(solution)/shard_map/psum | solution.py:271
  626.1 34.0 %all-reduce.9.cloned.1.call-done = (bf16[512,3,256]{2,0,1:T(8,128)(2,1)}, bf16[256,512]{1,0:T(8,128)(2,1)}, bf16[512,1024]{1,0:T(8,128)(2,1)}, bf16[1024,512]{1,0:T(8,128)(2,1)}) async-done(((bf16[512,3,256]{2,0,1:T(8,128)(2,1)}, bf16[256,512]{1,0:T(8,128)(2,1)}, bf16[512,1024]{1,0:T(8,128)(2,1)}, bf16[1024,512]{1,0:T(8,128)(2,1)}), (bf16[512,3,256]{2,0,1:T(8,128)(2,1)}, bf16[256,512]{1,0:T(8,128)(2,1)}, ...) | async-done | bytes 3145744 | tf_op jit(solution)/shard_map/psum | solution.py:281
  667.5 25.3 %reduce-scatter.23.cloned.1.call-done = f32[256,512]{1,0:T(8,128)} async-done(((f32[1024,512]{1,0:T(8,128)}), f32[256,512]{1,0:T(8,128)}) %reduce-scatter.23.cloned.1.call-update) | async-done | bytes 524304 | tf_op jit(solution)/shard_map/reduce_scatter | solution.py:62
  (159 shorter events, 87.5 us)
Async XLA Ops:
  7.2 239.7 %copy-start = (bf16[1024,512]{1,0:T(8,128)(2,1)S(1)}, bf16[1024,512]{1,0:T(8,128)(2,1)}, u32[]{:S(2)}) copy-start(bf16[1024,512]{1,0:T(8,128)(2,1)} %param.24) | copy-start | bytes 3145732
  7.2 21.8 %all-gather.8.cloned.1.call-start = ((), (), s32[]{:S(2)}) async-start(), calls=%async_computation.8 | async-start | bytes 1310720 | tf_op jit(solution)/shard_map/all_gather | solution.py:19
  7.9 68.6 %reduce-scatter.9.cloned.1.call-start = ((), (), s32[]{:S(2)}) async-start(), calls=%async_computation.9 | async-start | bytes 4718592 | tf_op jit(solution)/shard_map/reduce_scatter | solution.py:23
  33.0 92.6 %reduce-scatter.11.cloned.1.call-start = ((), (), s32[]{:S(2)}) async-start(), calls=%async_computation.10 | async-start | bytes 2621440 | tf_op jit(solution)/shard_map/reduce_scatter | solution.py:36
  92.4 33.2 %copy-start.28 = (f32[512]{0:T(512)S(1)}, f32[512]{0:T(512)}, u32[]{:S(2)}) copy-start(f32[512]{0:T(512)} %param.19) | copy-start | bytes 6148
  94.2 38.3 %copy-start.24 = (f32[512]{0:T(512)S(1)}, f32[512]{0:T(512)}, u32[]{:S(2)}) copy-start(f32[512]{0:T(512)} %param.20) | copy-start | bytes 6148
  94.2 38.3 %copy-start.26 = (f32[512]{0:T(512)S(1)}, f32[512]{0:T(512)}, u32[]{:S(2)}) copy-start(f32[512]{0:T(512)} %param.21) | copy-start | bytes 6148
  94.3 57.0 %all-gather.10.cloned.1.call-start = ((), (), s32[]{:S(2)}) async-start(), calls=%async_computation.11 | async-start | bytes 1310720 | tf_op jit(solution)/shard_map/all_gather | solution.py:19
  134.4 76.2 %reduce-scatter.13.cloned.1.call-start = ((), (), s32[]{:S(2)}) async-start(), calls=%async_computation.12 | async-start | bytes 6291456 | tf_op jit(solution)/shard_map/reduce_scatter | solution.py:23
  156.1 54.6 %copy-start.25 = (f32[1024]{0:T(1024)S(1)}, f32[1024]{0:T(1024)}, u32[]{:S(2)}) copy-start(f32[1024]{0:T(1024)} %param.23) | copy-start | bytes 12292
  156.1 90.8 %all-gather.12.cloned.1.call-start = ((), (), s32[]{:S(2)}) async-start(), calls=%async_computation.13 | async-start | bytes 3145728 | tf_op jit(solution)/shard_map/all_gather | solution.py:32
  213.7 68.8 %reduce-scatter.15.cloned.1.call-start = ((), (), s32[]{:S(2)}) async-start(), calls=%async_computation.14 | async-start | bytes 2621440 | tf_op jit(solution)/shard_map/reduce_scatter | solution.py:36
  251.1 38.5 %copy-start.27 = (f32[512]{0:T(512)S(1)}, f32[512]{0:T(512)}, u32[]{:S(2)}) copy-start(f32[512]{0:T(512)} %param.26) | copy-start | bytes 6148
  251.1 44.9 %copy-start.30 = (f32[512]{0:T(512)S(1)}, f32[512]{0:T(512)}, u32[]{:S(2)}) copy-start(f32[512]{0:T(512)} %param.27) | copy-start | bytes 6148
  251.1 65.4 %all-gather.14.cloned.1.call-start = ((), (), s32[]{:S(2)}) async-start(), calls=%async_computation.15 | async-start | bytes 1310720 | tf_op jit(solution)/shard_map/all_gather | solution.py:45
  299.6 75.9 %reduce-scatter.17.cloned.1.call-start = ((), (), s32[]{:S(2)}) async-start(), calls=%async_computation.16 | async-start | bytes 6291456 | tf_op jit(solution)/shard_map/reduce_scatter | solution.py:49
  320.9 91.3 %copy-start.34 = (bf16[512,1024]{1,0:T(8,128)(2,1)S(1)}, bf16[512,1024]{1,0:T(8,128)(2,1)}, u32[]{:S(2)}) copy-start(bf16[512,1024]{1,0:T(8,128)(2,1)} %param.22) | copy-start | bytes 3145732
  321.0 91.3 %all-gather.16.cloned.1.call-start = ((), (), s32[]{:S(2)}) async-start(), calls=%async_computation.17 | async-start | bytes 3145728 | tf_op jit(solution)/shard_map/all_gather | solution.py:58
  379.0 68.8 %reduce-scatter.19.cloned.1.call-start = ((), (), s32[]{:S(2)}) async-start(), calls=%async_computation.18 | async-start | bytes 2621440 | tf_op jit(solution)/shard_map/reduce_scatter | solution.py:62
  416.5 57.3 %all-gather.18.cloned.1.call-start = ((), (), s32[]{:S(2)}) async-start(), calls=%async_computation.19 | async-start | bytes 1310720 | tf_op jit(solution)/shard_map/all_gather | solution.py:45
  456.9 40.1 %reduce-scatter.21.cloned.1.call-start = ((), (), s32[]{:S(2)}) async-start(), calls=%async_computation.20 | async-start | bytes 1572864 | tf_op jit(solution)/shard_map/reduce_scatter | solution.py:49
  476.5 57.9 %all-gather.20.cloned.1.call-start = ((), (), s32[]{:S(2)}) async-start(), calls=%async_computation.21 | async-start | bytes 2359296 | tf_op jit(solution)/shard_map/all_gather | solution.py:58
  507.0 153.1 %all-reduce.9.cloned.1.call-start = ((), (), s32[]{:S(2)}) async-start(), calls=%async_computation.23 | async-start | bytes 6291456 | tf_op jit(solution)/shard_map/psum | solution.py:281
  537.9 154.9 %reduce-scatter.23.cloned.1.call-start = ((), (), s32[]{:S(2)}) async-start(), calls=%async_computation.22 | async-start | bytes 2621440 | tf_op jit(solution)/shard_map/reduce_scatter | solution.py:62
  (27 other events, 286.8 us)
Sparse Core Ops, SparseCore 0:
  9.6 19.4 all-gather.7
  33.1 43.4 reduce-scatter.8
  94.4 31.1 reduce-scatter.10
  134.6 16.6 all-gather.9
  156.2 54.3 reduce-scatter.12
  213.8 33.0 all-gather.11
  251.2 31.1 reduce-scatter.14
  299.7 16.7 all-gather.13
  321.1 54.3 reduce-scatter.16
  379.1 33.0 all-gather.15
  416.6 31.1 reduce-scatter.18
  457.0 16.7 all-gather.17
  476.6 20.3 reduce-scatter.20
  507.1 27.1 all-gather.19
  538.1 121.9 all-reduce.8
  662.4 30.3 reduce-scatter.22
where the time goes:
time: 702 us; the launch traced here: 701 us
  waiting for transfers between devices  482 us (69%)
  blocking collectives  113 us (16%)
  matrix products  45.8 us (7%)
  other arithmetic  35.5 us (5%)
  between operations  14.9 us (2%)
  local copies, waits for them, and re-layouts  9.27 us (1%)
    reduce_scatter x2, waiting for transfers between devices, forward_reduce(): lax.psum_scatter(product_term(jnp.int32(0), row_count * lax.axis_size('ro...  97.2 us
    reduce_scatter x2, waiting for transfers between devices, backward_reduce(): lax.psum_scatter(product_term(jnp.int32(0), row_count * lax.axis_size('ro...  74.9 us
    psum x1, blocking collectives, shards(): lax.psum((jnp.sum(first_norm_gradient, axis=0), jnp.sum(norm_gradient_tot...  65 us
    reduce_scatter x2, waiting for transfers between devices, forward_combine(): lax.psum_scatter(product_term(jnp.int32(0), row_count * lax.axis_size('co...  62.6 us
    reduce_scatter x2, waiting for transfers between devices, backward_combine(): lax.psum_scatter(product_term(jnp.int32(0), row_count * lax.axis_size('co...  56.5 us
    all_gather x2, waiting for transfers between devices, backward_collect(): return lax.all_gather(block, 'row', axis=0, tiled=True)  52.5 us
    all_gather x2, waiting for transfers between devices, forward_gather(): return lax.all_gather(block, 'col', axis=0, tiled=True)  36.4 us
    psum x1, waiting for transfers between devices, shards(): lax.psum(grad_qkv.astype(jnp.bfloat16), 'dp').astype(jnp.float32)  34 us
  transfers between devices with their start and end apart: 16, of which 16 were waited for; matrix products, arithmetic and copies ran while one was open for 3% of the time, Pallas kernels for 0%

commit v1 on v0

v1 whole, which is shorter than its diff:
```python
import jax
import jax.numpy as jnp
from jax import lax
from jax.experimental import pallas as pl
from jax.experimental.pallas import tpu as pltpu
from jax.sharding import PartitionSpec as P

MODEL_WIDTH = 1024
HEADS = 16
HEAD_DIM = 64
L = 512


norm_epsilon = 1e-12
masked_score = -1e30
root_half = 0.7071067811865476
gauss_height = 0.3989422804014327


def chip_steps(rows, cols):
    steps = [(dr, dc) for dr in range(rows) for dc in range(0, cols, 2)]
    return steps[::-1]


def greet(peers):
    barrier = pltpu.get_barrier_semaphore()
    for peer in peers:
        pl.semaphore_signal(barrier, inc=1, device_id=peer)
    pl.semaphore_wait(barrier, len(peers))


def place(row, col):
    return {"row": row, "col": col}


def send(source, target, send_sem, recv_sem, peer):
    return pltpu.make_async_remote_copy(
        src_ref=source, dst_ref=target, send_sem=send_sem, recv_sem=recv_sem, device_id=peer
    )


def block_of(ref, tiled, rows, cols, row, col):
    if tiled:
        high, wide = ref.shape[0] // cols, ref.shape[1] // rows
        return ref.at[
            pl.ds(pl.multiple_of(col * high, high), high),
            pl.ds(pl.multiple_of(row * wide, wide), wide),
        ]
    high = ref.shape[0] // (rows * cols)
    return ref.at[pl.ds(pl.multiple_of((col * rows + row) * high, high), high), :]


def gather_kernel(tiled, x_ref, out_ref, far_send, far_recv, near_send, near_recv):
    rows, cols = lax.axis_size("row"), lax.axis_size("col")
    r, c = lax.axis_index("row"), lax.axis_index("col")
    mate = c + 1 - 2 * (c % 2)
    steps = chip_steps(rows, cols)
    view = lambda row, col: block_of(out_ref, tiled, rows, cols, row, col)
    greet([place((r + dr) % rows, (c + dc) % cols) for dr, dc in steps[:-1]] + [place(r, mate)])
    copies = []
    for i, (dr, dc) in enumerate(steps[:-1]):
        copies.append(
            send(
                x_ref,
                view(r, c),
                far_send.at[i],
                far_recv.at[i],
                place((r + dr) % rows, (c + dc) % cols),
            )
        )
        copies[-1].start()
    last = len(steps) - 1
    near = [send(x_ref, view(r, c), near_send.at[last], near_recv.at[last], place(r, mate))]
    near[0].start()
    view(r, c)[...] = x_ref[...]
    for i in list(range(1, last)) + [0] if last > 0 else []:
        dr, dc = steps[i]
        row, col = (r - dr + rows) % rows, (c - dc + cols) % cols
        pltpu.make_async_remote_copy(
            src_ref=x_ref,
            dst_ref=view(row, col),
            send_sem=far_send.at[i],
            recv_sem=far_recv.at[i],
            device_id=place(r, mate),
        ).wait_recv()
        near.append(
            send(view(row, col), view(row, col), near_send.at[i], near_recv.at[i], place(r, mate))
        )
        near[-1].start()
    for i, (dr, dc) in enumerate(steps):
        row, col = (r - dr + rows) % rows, (mate - dc + cols) % cols
        pltpu.make_async_remote_copy(
            src_ref=x_ref,
            dst_ref=view(row, col),
            send_sem=near_send.at[i],
            recv_sem=near_recv.at[i],
            device_id=place(r, mate),
        ).wait_recv()
    for copy in copies + near:
        copy.wait_send()


def vmem_spec():
    return pl.BlockSpec(memory_space=pltpu.VMEM)


def gather_blocks(block, tiled, key):
    rows, cols = lax.axis_size("row"), lax.axis_size("col")
    count = rows * cols // 2
    shape = (
        (block.shape[0] * cols, block.shape[1] * rows)
        if tiled
        else (block.shape[0] * rows * cols, block.shape[1])
    )
    return pl.pallas_call(
        lambda *refs: gather_kernel(tiled, *refs),
        out_shape=jax.ShapeDtypeStruct(shape, block.dtype),
        in_specs=[vmem_spec()],
        out_specs=vmem_spec(),
        scratch_shapes=[pltpu.SemaphoreType.DMA((count,))] * 4,
        cost_estimate=pl.CostEstimate(flops=0, bytes_accessed=30000000, transcendentals=0),
        compiler_params=pltpu.CompilerParams(collective_id=key, has_side_effects=True),
        name=f"gather_{key}",
    )(block)


def reduce_kernel(
    tiled,
    turned,
    a_ref,
    b_ref,
    out_ref,
    near_out,
    near_in,
    far_out,
    far_in,
    near_send,
    near_recv,
    far_send,
    far_recv,
):
    rows, cols = lax.axis_size("row"), lax.axis_size("col")
    r, c = lax.axis_index("row"), lax.axis_index("col")
    flip = 1 - 2 * (c % 2)
    mate = c + flip
    steps = chip_steps(rows, cols)
    high, wide = out_ref.shape
    last = len(steps) - 1
    greet([place((r + dr) % rows, (c + dc) % cols) for dr, dc in steps[:-1]] + [place(r, mate)])

    def part(row, col):
        if tiled:
            left = a_ref[pl.ds(pl.multiple_of(col * high, high), high), :]
            right = b_ref[pl.ds(pl.multiple_of(row * wide, wide), wide), :]
        else:
            left = a_ref[pl.ds(pl.multiple_of((col * rows + row) * high, high), high), :]
            right = b_ref[...]
        return lax.dot_general(
            left,
            right,
            (((1,), (1 if turned else 0,)), ((), ())),
            preferred_element_type=jnp.float32,
        )

    copies = []
    for i, (dr, dc) in enumerate(steps):
        row, col = (r + dr) % rows, (c + dc) % cols
        near_out[i] = part(row, col + flip).astype(jnp.bfloat16)
        copies.append(
            send(near_out.at[i], near_in.at[i], near_send.at[i], near_recv.at[i], place(r, mate))
        )
        copies[-1].start()
    near = list(copies)
    far = []
    for i, (dr, dc) in enumerate(steps):
        row, col = (r + dr) % rows, (c + dc) % cols
        total = part(row, col)
        near[i].wait_recv()
        total = total + near_in[i].astype(jnp.float32)
        if i < last:
            far_out[i] = total.astype(jnp.bfloat16)
            far.append(
                send(far_out.at[i], far_in.at[i], far_send.at[i], far_recv.at[i], place(row, col))
            )
            far[-1].start()
        else:
            out_ref[...] = total
    for i in list(range(1, last)) + [0] if last > 0 else []:
        far[i].wait_recv()
        out_ref[...] += far_in[i].astype(jnp.float32)
    for copy in near + far:
        copy.wait_send()


def reduce_blocks(a, b, tiled, turned, key):
    rows, cols = lax.axis_size("row"), lax.axis_size("col")
    count = rows * cols // 2
    width = b.shape[0] if turned else b.shape[1]
    shape = (a.shape[0] // cols, width // rows) if tiled else (a.shape[0] // (rows * cols), width)
    slots = lambda n: pltpu.VMEM((n,) + shape, jnp.bfloat16)
    return pl.pallas_call(
        lambda *refs: reduce_kernel(tiled, turned, *refs),
        out_shape=jax.ShapeDtypeStruct(shape, jnp.float32),
        in_specs=[vmem_spec()] * 2,
        out_specs=vmem_spec(),
        scratch_shapes=[slots(count), slots(count), slots(count - 1), slots(count - 1)]
        + [pltpu.SemaphoreType.DMA((count,))] * 4,
        cost_estimate=pl.CostEstimate(
            flops=2 * a.shape[0] * a.shape[1] * width, bytes_accessed=40000000, transcendentals=0
        ),
        compiler_params=pltpu.CompilerParams(collective_id=key, has_side_effects=True),
        name=f"reduce_{key}",
    )(a, b)


def turn_kernel(x_ref, out_ref, send_sem, recv_sem):
    rows, cols = lax.axis_size("row"), lax.axis_size("col")
    r, c = lax.axis_index("row"), lax.axis_index("col")
    high, wide = out_ref.shape[0], x_ref.shape[1]
    steps = [(dr, dc) for dr in range(rows) for dc in range(cols)][1:]

    def source(row, col):
        return x_ref.at[pl.ds(pl.multiple_of((col * rows + row) * high, high), high), :]

    def target(row, col):
        return out_ref.at[:, pl.ds(pl.multiple_of((col * rows + row) * wide, wide), wide)]

    greet([place((r + dr) % rows, (c + dc) % cols) for dr, dc in steps])
    copies = []
    for i, (dr, dc) in enumerate(steps):
        row, col = (r + dr) % rows, (c + dc) % cols
        copies.append(
            send(source(row, col), target(r, c), send_sem.at[i], recv_sem.at[i], place(row, col))
        )
        copies[-1].start()
    target(r, c)[...] = source(r, c)[...]
    for i, (dr, dc) in enumerate(steps):
        row, col = (r - dr + rows) % rows, (c - dc + cols) % cols
        send(
            source(r, c), target(row, col), send_sem.at[i], recv_sem.at[i], place(row, col)
        ).wait_recv()
    for copy in copies:
        copy.wait_send()


def turn_blocks(x, key):
    group = lax.axis_size("row") * lax.axis_size("col")
    return pl.pallas_call(
        turn_kernel,
        out_shape=jax.ShapeDtypeStruct((x.shape[0] // group, x.shape[1] * group), x.dtype),
        in_specs=[vmem_spec()],
        out_specs=vmem_spec(),
        scratch_shapes=[pltpu.SemaphoreType.DMA((group - 1,))] * 2,
        cost_estimate=pl.CostEstimate(flops=0, bytes_accessed=10000000, transcendentals=0),
        compiler_params=pltpu.CompilerParams(collective_id=key, has_side_effects=True),
        name=f"turn_{key}",
    )(x)


def depth_kernel(x_ref, out_ref, send_sem, recv_sem):
    depth = lax.axis_size("dp")
    d = lax.axis_index("dp")
    greet([{"dp": (d + i) % depth} for i in range(1, depth)])
    copies = []
    for i in range(1, depth):
        copies.append(
            send(
                x_ref,
                out_ref.at[d],
                send_sem.at[i - 1],
                recv_sem.at[i - 1],
                {"dp": (d + i) % depth},
            )
        )
        copies[-1].start()
    out_ref[d] = x_ref[...]
    for i in range(1, depth):
        origin = (d - i + depth) % depth
        send(
            x_ref, out_ref.at[origin], send_sem.at[i - 1], recv_sem.at[i - 1], {"dp": origin}
        ).wait_recv()
    for copy in copies:
        copy.wait_send()


def depth_sum(x, key):
    depth = lax.axis_size("dp")
    stacked = pl.pallas_call(
        depth_kernel,
        out_shape=jax.ShapeDtypeStruct((depth,) + x.shape, x.dtype),
        in_specs=[vmem_spec()],
        out_specs=vmem_spec(),
        scratch_shapes=[pltpu.SemaphoreType.DMA((depth - 1,))] * 2,
        cost_estimate=pl.CostEstimate(flops=0, bytes_accessed=10000000, transcendentals=0),
        compiler_params=pltpu.CompilerParams(collective_id=key, has_side_effects=True),
        name=f"depth_{key}",
    )(x)
    return jnp.sum(stacked, axis=0)


def swap(x, split, join):
    if lax.axis_size("row") != 2:
        return lax.all_to_all(x, "row", split, join, tiled=True)
    r = lax.axis_index("row")
    half = x.shape[split] // 2
    kept = lax.dynamic_slice_in_dim(x, r * half, half, split)
    given = lax.dynamic_slice_in_dim(x, (1 - r) * half, half, split)
    taken = lax.ppermute(given, "row", [(0, 1), (1, 0)])
    low = jnp.where(r == 0, kept, taken)
    high = jnp.where(r == 0, taken, kept)
    return jnp.concatenate([low, high], axis=join)


def widen_rows(x, axis):
    if lax.axis_size("row") != 2:
        return lax.all_gather(x, "row", axis=axis, tiled=True)
    r = lax.axis_index("row")
    other = lax.ppermute(x, "row", [(0, 1), (1, 0)])
    return jnp.concatenate([jnp.where(r == 0, x, other), jnp.where(r == 0, other, x)], axis=axis)


def contract_rows(first_side, second_side):
    return lax.dot_general(
        first_side, second_side, (((0,), (0,)), ((), ())), preferred_element_type=jnp.float32
    )


def gelu_pair(preact):
    lower_mass = 0.5 * (1.0 + lax.erf(preact * root_half))
    return (
        preact * lower_mass,
        lower_mass + preact * jnp.exp(-0.5 * preact * preact) * gauss_height,
    )


def norm_forward(hidden, norm_gain, norm_shift):
    center = jnp.sum(hidden, axis=-1, keepdims=True) / MODEL_WIDTH
    square = jnp.sum(hidden * hidden, axis=-1, keepdims=True) / MODEL_WIDTH
    rscale = lax.rsqrt(square - center * center + norm_epsilon)
    normed = (hidden - center) * rscale
    return (normed * norm_gain + norm_shift, normed, rscale)


def norm_back(incoming_gradient, normed, rscale, norm_gain):
    scaled = incoming_gradient * norm_gain
    first_mean = jnp.sum(scaled, axis=-1, keepdims=True)
    second_mean = jnp.sum(scaled * normed, axis=-1, keepdims=True)
    return rscale * (scaled - first_mean / MODEL_WIDTH - normed * (second_mean / MODEL_WIDTH))


def score_block(queries, keys_low, lengths):
    scores = jnp.einsum(
        "sqhd,skhd->shqk", queries, keys_low, preferred_element_type=jnp.float32
    ) * HEAD_DIM ** (-0.5)
    visible = lax.broadcasted_iota(jnp.int32, (1, 1, 1, L), 3) < lengths[:, None, None, None]
    return jnp.where(visible, scores, masked_score)


def attend(queries, keys_low, values, lengths):
    scores = score_block(queries, keys_low, lengths)
    row_peak = jnp.max(scores, axis=3, keepdims=True)
    logsum = row_peak + jnp.log(jnp.sum(jnp.exp(scores - row_peak), axis=3, keepdims=True))
    soft_weights = jnp.exp(scores - logsum).astype(jnp.bfloat16)
    attention_output = jnp.einsum(
        "shqk,skhd->sqhd", soft_weights, values, preferred_element_type=jnp.float32
    )
    return (attention_output.astype(jnp.bfloat16), logsum)


def attend_back(queries, keys_low, values, logsum, incoming_gradient, lengths):
    scores = score_block(queries, keys_low, lengths)
    soft_weights = jnp.exp(scores - logsum)
    grad_weights = jnp.einsum(
        "sqhd,skhd->shqk", incoming_gradient, values, preferred_element_type=jnp.float32
    )
    row_inner = jnp.sum(soft_weights * grad_weights, axis=3, keepdims=True)
    score_grad = (soft_weights * (grad_weights - row_inner)).astype(jnp.bfloat16)
    score_scale = HEAD_DIM ** (-0.5)
    grad_queries = (
        jnp.einsum("shqk,skhd->sqhd", score_grad, keys_low, preferred_element_type=jnp.float32)
        * score_scale
    )
    grad_keys = (
        jnp.einsum("shqk,sqhd->skhd", score_grad, queries, preferred_element_type=jnp.float32)
        * score_scale
    )
    grad_values = jnp.einsum(
        "shqk,sqhd->skhd",
        soft_weights.astype(jnp.bfloat16),
        incoming_gradient,
        preferred_element_type=jnp.float32,
    )
    return (grad_queries, grad_keys, grad_values)


def shards(
    inputs,
    qkv_weight,
    qv_bias,
    out_weight,
    out_bias,
    first_gain,
    first_shift,
    up_weight,
    up_bias,
    down_weight,
    down_bias,
    second_gain,
    second_shift,
    lengths,
    out_grad,
):
    rows, cols = lax.axis_size("row"), lax.axis_size("col")
    r, c = lax.axis_index("row"), lax.axis_index("col")
    group = rows * cols
    g = c * rows + r
    bf16 = jnp.bfloat16

    def part(x, index, count, axis):
        size = x.shape[axis] // count
        return lax.dynamic_slice_in_dim(x, index * size, size, axis)

    qkv_full = swap(qkv_weight, 2, 0)
    lane = qkv_full.shape[2]
    qkv_flat = qkv_full.reshape(qkv_full.shape[0], -1)
    all_lengths = widen_rows(lengths, 0)
    seqs = all_lengths.shape[0]
    head_shape = (seqs, L, HEADS // group, HEAD_DIM)
    gathered_in = gather_blocks(inputs, True, 0)
    tokens = gathered_in.shape[0]
    vectors = widen_rows(
        jnp.stack([out_bias, first_gain, first_shift, down_bias, second_gain, second_shift]), 1
    )
    out_bias, first_gain, first_shift, down_bias, second_gain, second_shift = [
        vectors[i] for i in range(6)
    ]
    out_full = lax.all_gather(
        lax.all_gather(out_weight, "row", axis=1, tiled=True), "col", axis=0, tiled=True
    )
    up_full = swap(up_weight, 1, 0)
    down_full = swap(down_weight, 0, 1)
    incoming_gradient = swap(out_grad, 0, 1).astype(jnp.float32)
    qv_own = part(qv_bias, r, rows, 1)
    up_own = part(up_bias, r, rows, 0)

    projected = jnp.dot(gathered_in, qkv_flat, preferred_element_type=jnp.float32).reshape(
        tokens, 3, lane
    )
    queries = (projected[:, 0] + qv_own[0]).astype(bf16).reshape(head_shape)
    keys_low = projected[:, 1].astype(bf16).reshape(head_shape)
    values = (projected[:, 2] + qv_own[1]).astype(bf16).reshape(head_shape)
    attention_output, logsum = attend(queries, keys_low, values, all_lengths)
    attended = attention_output.reshape(tokens, lane)
    turned_att = turn_blocks(attended, 1)
    first_sum = (
        part(gathered_in, g, group, 0).astype(jnp.float32)
        + jnp.dot(turned_att, out_full, preferred_element_type=jnp.float32)
        + out_bias
    )
    first_norm, first_standardized, first_scale = norm_forward(first_sum, first_gain, first_shift)
    gathered_norm = gather_blocks(first_norm.astype(bf16), False, 2)
    preact = jnp.dot(gathered_norm, up_full, preferred_element_type=jnp.float32) + up_own
    activated, gelu_slope = gelu_pair(preact)
    activated = activated.astype(bf16)
    second_sum = first_norm + reduce_blocks(activated, down_full, False, False, 3) + down_bias
    second_norm, second_standardized, second_scale = norm_forward(
        second_sum, second_gain, second_shift
    )
    block_out = swap(second_norm.astype(bf16), 1, 0)
    second_norm_gradient = norm_back(
        incoming_gradient, second_standardized, second_scale, second_gain
    )
    gathered_grad = gather_blocks(second_norm_gradient.astype(bf16), False, 4)
    grad_down = swap(contract_rows(activated, gathered_grad).astype(bf16), 1, 0)
    grad_down = lax.psum(grad_down, "dp")
    preactivation_gradient = (
        lax.dot_general(
            gathered_grad,
            down_full,
            (((1,), (1,)), ((), ())),
            preferred_element_type=jnp.float32,
        )
        * gelu_slope
    )
    pre_low = preactivation_gradient.astype(bf16)
    grad_up = swap(contract_rows(gathered_norm, pre_low).astype(bf16), 0, 1)
    norm_gradient_total = second_norm_gradient + reduce_blocks(pre_low, up_full, False, True, 5)
    grad_up, grad_down = lax.optimization_barrier((grad_up, grad_down))
    grad_up = lax.psum(grad_up, "dp")
    first_norm_gradient = norm_back(
        norm_gradient_total, first_standardized, first_scale, first_gain
    )
    gathered_first = gather_blocks(first_norm_gradient.astype(bf16), False, 6)
    grad_out = swap(contract_rows(attended, gathered_first).astype(bf16), 1, 0)
    attended_grad = (
        lax.dot_general(
            gathered_first,
            part(out_full, g, group, 0),
            (((1,), (1,)), ((), ())),
            preferred_element_type=jnp.float32,
        )
        .astype(bf16)
        .reshape(head_shape)
    )
    grad_queries, grad_keys, grad_values = attend_back(
        queries, keys_low, values, logsum, attended_grad, all_lengths
    )
    query_rows_flattened = grad_queries.reshape(tokens, -1)
    value_rows_flattened = grad_values.reshape(tokens, -1)
    combined_heads = jnp.concatenate(
        [query_rows_flattened, grad_keys.reshape(tokens, -1), value_rows_flattened], axis=1
    ).astype(bf16)
    grad_qkv = swap(
        contract_rows(gathered_in, combined_heads).astype(bf16).reshape(qkv_full.shape), 0, 2
    )
    grad_qkv, grad_out, grad_up = lax.optimization_barrier((grad_qkv, grad_out, grad_up))
    grad_qkv = lax.psum(grad_qkv, "dp")
    grad_out = lax.psum(grad_out, "dp")
    first_tile = swap(first_norm_gradient, 1, 0)
    grad_inputs = first_tile + reduce_blocks(combined_heads, qkv_flat, True, True, 7)
    column_part = jnp.stack(
        [
            jnp.sum(first_norm_gradient, axis=0),
            jnp.sum(norm_gradient_total * first_standardized, axis=0),
            jnp.sum(norm_gradient_total, axis=0),
            jnp.sum(second_norm_gradient, axis=0),
            jnp.sum(incoming_gradient * second_standardized, axis=0),
            jnp.sum(incoming_gradient, axis=0),
        ]
    )
    hidden_sum = jnp.sum(preactivation_gradient, axis=0)
    query_sum = jnp.sum(query_rows_flattened, axis=0)
    value_sum = jnp.sum(value_rows_flattened, axis=0)
    width = column_part.shape[1]
    loose = jnp.concatenate([hidden_sum, query_sum, value_sum])
    lines = -(-loose.shape[0] // width)
    lines = -(-(6 + lines) // 8) * 8 - 6
    loose = jnp.pad(loose, (0, lines * width - loose.shape[0])).reshape(lines, width)
    spread = gather_blocks(jnp.concatenate([column_part, loose]), False, 8)
    spread = spread.reshape(cols, rows, 6 + lines, width)
    column_all = jnp.sum(spread[:, :, :6], axis=(0, 1))
    loose_all = lax.dynamic_index_in_dim(spread[:, :, 6:], c, 0, keepdims=False)
    loose_all = loose_all.reshape(rows, lines * width)
    units = hidden_sum.shape[0]
    packed = jnp.concatenate(
        [
            part(column_all, r, rows, 1).reshape(-1),
            loose_all[:, :units].reshape(-1),
            loose_all[:, units : units + lane].reshape(-1),
            loose_all[:, units + lane : units + 2 * lane].reshape(-1),
        ]
    )
    size = packed.shape[0]
    packed = jnp.pad(packed, (0, -size % 1024)).reshape(-1, 128)
    packed = depth_sum(packed, 9).reshape(-1)
    half = width // rows
    column_sums = packed[: 6 * half].reshape(6, half)
    hidden_total = packed[6 * half : 6 * half + rows * units]
    qv_total = packed[6 * half + rows * units : size].reshape(2, rows * lane)
    return (
        block_out,
        grad_inputs,
        grad_qkv.astype(jnp.float32),
        qv_total,
        grad_out.astype(jnp.float32),
        column_sums[0],
        column_sums[1],
        column_sums[2],
        grad_up.astype(jnp.float32),
        hidden_total,
        grad_down.astype(jnp.float32),
        column_sums[3],
        column_sums[4],
        column_sums[5],
    )


def solution(mesh):
    in_specs = (
        P(("dp", "col"), "row"),
        P("row", None, "col"),
        P(None, "col"),
        P("col", "row"),
        P("row"),
        P("row"),
        P("row"),
        P("row", "col"),
        P("col"),
        P("col", "row"),
        P("row"),
        P("row"),
        P("row"),
        P(("dp", "row")),
        P(("dp", "col"), "row"),
    )
    out_specs = (
        P(("dp", "col"), "row"),
        P(("dp", "col"), "row"),
        P("row", None, "col"),
        P(None, "col"),
        P("col", "row"),
        P("row"),
        P("row"),
        P("row"),
        P("row", "col"),
        P("col"),
        P("col", "row"),
        P("row"),
        P("row"),
        P("row"),
    )
    return jax.shard_map(shards, mesh=mesh, in_specs=in_specs, out_specs=out_specs, check_vma=False)
```

time: 702 us -> 454 us (0.65)
  waiting for transfers between devices: 482 us -> 115 us
  Pallas kernels: 0 us -> 176 us
  blocking collectives: 113 us -> 11.8 us
  local copies, waits for them, and re-layouts: 9.27 us -> 43.2 us
  starting transfers between devices: 0.84 us -> 15.4 us
  matrix products: 45.8 us -> 36.4 us
    reduce_scatter x8 -> x0, waiting for transfers between devices: 291 us -> none  [the longest x2 97.2 us: forward_reduce(): lax.psum_scatter(product_term(jnp.int32(0), row_count * lax.axis_size('ro...]
    pallas_call x0 -> x10, Pallas kernels: none -> 176 us  [the longest x5 101 us: gather_blocks(): pl.pallas_call(lambda *refs: gather_kernel(tiled, *refs), out_shape=jax.S...]
    all_gather x7 -> x1, waiting for transfers between devices: 156 us -> 0.01 us  [shards(): lax.all_gather(lax.all_gather(out_weight, 'row', axis=1, tiled=True), 'co...]
    psum x6 -> x0, blocking collectives: 105 us -> none  [the longest x1 65 us: shards(): lax.psum((jnp.sum(first_norm_gradient, axis=0), jnp.sum(norm_gradient_tot...]
    psum x1 -> x3, waiting for transfers between devices: 34 us -> 99.5 us  [the longest x1 42.2 us: shards(): grad_up = lax.psum(grad_up, 'dp')]
    ppermute x0 -> x12, waiting for transfers between devices: none -> 15.4 us  [the longest x10 15.3 us: swap(): taken = lax.ppermute(given, 'row', [(0, 1), (1, 0)])]
    ppermute x0 -> x12, starting transfers between devices: none -> 15 us  [the longest x10 12.9 us: swap(): taken = lax.ppermute(given, 'row', [(0, 1), (1, 0)])]
    dot_general x8 -> x5, matrix products: 28.3 us -> 15.8 us  [the longest x1 6.03 us: shards(): lax.dot_general(gathered_grad, down_full, (((1,), (1,)), ((), ())), prefe...]
  transfers between devices with their start and end apart: 16 -> 16, of which waited for: 16 -> 6; matrix products, arithmetic and copies ran while one was open for 3% -> 15% of each run, Pallas kernels for 0% -> 17%
where the time goes in v1:
time: 454 us; the launch traced here: 452 us
  Pallas kernels  176 us (39%)
  waiting for transfers between devices  115 us (25%)
  local copies, waits for them, and re-layouts  43.2 us (10%)
  other arithmetic  38.2 us (8%)
  matrix products  36.4 us (8%)
  between operations  16.6 us (4%)
  starting transfers between devices  15.4 us (3%)
  blocking collectives  11.8 us (3%)
    pallas_call x5, Pallas kernels, gather_blocks(): pl.pallas_call(lambda *refs: gather_kernel(tiled, *refs), out_shape=jax.S...  101 us
    pallas_call x3, Pallas kernels, reduce_blocks(): pl.pallas_call(lambda *refs: reduce_kernel(tiled, turned, *refs), out_sha...  59.8 us
    psum x1, waiting for transfers between devices, shards(): grad_up = lax.psum(grad_up, 'dp')  42.2 us
    psum x1, waiting for transfers between devices, shards(): grad_down = lax.psum(grad_down, 'dp')  31.7 us
    psum x1, waiting for transfers between devices, shards(): grad_qkv = lax.psum(grad_qkv, 'dp')  25.6 us
    ppermute x10, waiting for transfers between devices, swap(): taken = lax.ppermute(given, 'row', [(0, 1), (1, 0)])  15.3 us
    ppermute x10, starting transfers between devices, swap(): taken = lax.ppermute(given, 'row', [(0, 1), (1, 0)])  12.9 us
    all_gather x1, blocking collectives, shards(): lax.all_gather(out_weight, 'row', axis=1, tiled=True)  11.8 us
  transfers between devices with their start and end apart: 16, of which 6 were waited for; matrix products, arithmetic and copies ran while one was open for 15% of the time, Pallas kernels for 17%

profile of v1, /device:TPU:0, one launch (start us, length us, event | category | flops | bytes accessed | tf_op | source)
XLA Modules:
  0.0 452.3 jit_solution(14313474353994500786)
XLA Ops:
  8.8 3.0 collective-permute-start
  15.2 11.8 %all_gather.6 = bf16[256,1024]{1,0:T(8,128)(2,1)} all-gather(bf16[256,512]{1,0:T(8,128)(2,1)S(1)} %copy-done.40), channel_id=1, replica_groups=mesh['dp'=4,'row'=2,'col'=4] {'row'}, dimensions={1}, use_global_device_ids=true | all-gather | bytes 786432 | tf_op jit(solution)/shard_map/all_gather | solution.py:438
  31.7 35.5 %gather_0.1 = bf16[1024,1024]{1,0:T(8,128)(2,1)} custom-call(bf16[256,512]{1,0:T(8,128)(2,1)} %refs_0_.1), custom_call_target="tpu_custom_call" | custom-call | bytes 30000000 | tf_op jit(solution)/shard_map/gather_0/pallas_call | solution.py:115
  94.1 8.2 %turn_1.1 = bf16[128,1024]{1,0:T(8,128)(2,1)} custom-call(bf16[1024,128]{1,0:T(8,128)(2,1)} %copy.76.x_ref), custom_call_target="tpu_custom_call" | custom-call | bytes 10000000 | tf_op jit(solution)/shard_map/turn_1/pallas_call | solution.py:248
  112.1 19.3 %gather_2.1 = bf16[1024,1024]{1,0:T(8,128)(2,1)} custom-call(bf16[128,1024]{1,0:T(8,128)(2,1)} %fusion.20.refs_0_), custom_call_target="tpu_custom_call" | custom-call | bytes 30000000 | tf_op jit(solution)/shard_map/gather_2/pallas_call | solution.py:115
  131.5 4.7 %multiply_convert_fusion.1 = (bf16[1024,512]{1,0:T(8,128)(2,1)}, f32[1024,512]{1,0:T(8,128)}) fusion(f32[512]{0:T(512)} %dynamic_slice.85, bf16[1024,1024]{1,0:T(8,128)(2,1)} %gather_2.1, bf16[512,512]{1,0:T(8,128)(2,1)} %copy-done.21, bf16[512,512]{1,0:T(8,128)(2,1)S(1)} %copy-done.20), kind=kOutput, calls=%fused_computation.13 | convolution fusion | flops 1078984704 | bytes 6293504 | tf_op jit(solution)/shard_map/dot_general | solution.py:462
  136.2 19.9 %reduce_3.1 = f32[128,1024]{1,0:T(8,128)} custom-call(bf16[1024,512]{1,0:T(8,128)(2,1)} %get-tuple-element.129.refs_0_, bf16[512,1024]{1,0:T(8,128)(2,1)} %pad_maximum_fusion.1.refs_1_), custom_call_target="tpu_custom_call" | custom-call | flops 1073741824 | bytes 40000000 | tf_op jit(solution)/shard_map/reduce_3/pallas_call | solution.py:201
  160.8 18.8 %gather_4.1 = bf16[1024,1024]{1,0:T(8,128)(2,1)} custom-call(bf16[128,1024]{1,0:T(8,128)(2,1)} %convert_element_type.96.refs_0_), custom_call_target="tpu_custom_call" | custom-call | bytes 30000000 | tf_op jit(solution)/shard_map/gather_4/pallas_call | solution.py:115
  179.6 6.0 %fusion.43 = (f32[512]{0:T(512)}, bf16[1024,512]{1,0:T(8,128)(2,1)}) fusion(f32[1024,512]{1,0:T(8,128)} %get-tuple-element.130, f32[512]{0:T(512)S(1)} %copy-done.64, bf16[1024,1024]{1,0:T(8,128)(2,1)} %gather_4.1, bf16[512,512]{1,0:T(8,128)(2,1)} %copy-done.18, bf16[512,512]{1,0:T(8,128)(2,1)} %copy-done.17), kind=kOutput, calls=%fused_computation.158 | convolution fusion | flops 1082129920 | bytes 6295552 | tf_op jit(solution)/shard_map/dot_general | solution.py:477
  185.7 20.2 %reduce_5.1 = f32[128,1024]{1,0:T(8,128)} custom-call(bf16[1024,512]{1,0:T(8,128)(2,1)} %get-tuple-element.75.refs_0_, bf16[1024,512]{1,0:T(8,128)(2,1)} %pad_maximum_fusion.refs_1_), custom_call_target="tpu_custom_call" | custom-call | flops 1073741824 | bytes 40000000 | tf_op jit(solution)/shard_map/reduce_5/pallas_call | solution.py:201
  209.4 18.7 %gather_6.1 = bf16[1024,1024]{1,0:T(8,128)(2,1)} custom-call(bf16[128,1024]{1,0:T(8,128)(2,1)} %convert_element_type.98.refs_0_), custom_call_target="tpu_custom_call" | custom-call | bytes 30000000 | tf_op jit(solution)/shard_map/gather_6/pallas_call | solution.py:115
  228.1 2.9 convolution_convert_fusion.3
  235.1 3.7 multiply_reduce_fusion
  242.8 2.5 fusion.46
  264.7 2.4 collective-permute-done.11
  267.1 11.2 %collective-permute-done.10 = bf16[512,512]{1,0:T(8,128)(2,1)} collective-permute-done((bf16[512,512]{1,0:T(8,128)(2,1)}, bf16[512,512]{1,0:T(8,128)(2,1)}, u32[]{:S(2)}, u32[]{:S(2)}) %collective-permute-start.10) | collective-permute-done | bytes 524320 | tf_op jit(solution)/shard_map/ppermute | solution.py:308
  278.3 2.4 broadcast_select_fusion.1
  290.4 8.6 %gather_8.1 = f32[64,1024]{1,0:T(8,128)} custom-call(f32[8,1024]{1,0:T(8,128)} %concatenate.63.refs_0_), custom_call_target="tpu_custom_call" | custom-call | bytes 30000000 | tf_op jit(solution)/shard_map/gather_8/pallas_call | solution.py:115
  302.4 31.7 %all-reduce.7.cloned.1.call-done = bf16[1024,512]{1,0:T(8,128)(2,1)} async-done(((bf16[1024,512]{1,0:T(8,128)(2,1)}), bf16[1024,512]{1,0:T(8,128)(2,1)}) %all-reduce.7.cloned.1.call-update) | async-done | bytes 1048592 | tf_op jit(solution)/shard_map/psum | solution.py:475
  335.1 7.0 %depth_9.1 = f32[4,40,128]{2,1,0:T(8,128)} custom-call(f32[40,128]{1,0:T(8,128)} %fusion.32.x_ref), custom_call_target="tpu_custom_call" | custom-call | bytes 10000000 | tf_op jit(solution)/shard_map/depth_9/pallas_call | solution.py:288
  346.0 42.2 %all-reduce.9.cloned.1.call-done = bf16[512,1024]{1,0:T(8,128)(2,1)} async-done(((bf16[512,1024]{1,0:T(8,128)(2,1)}), bf16[512,1024]{1,0:T(8,128)(2,1)}) %all-reduce.9.cloned.1.call-update) | async-done | bytes 1048592 | tf_op jit(solution)/shard_map/psum | solution.py:489
  390.0 19.7 %reduce_7.1 = f32[256,512]{1,0:T(8,128)} custom-call(bf16[1024,384]{1,0:T(8,128)(2,1)} %copy-done.22, bf16[1024,384]{1,0:T(8,128)(2,1)} %copy.90.refs_1_), custom_call_target="tpu_custom_call" | custom-call | flops 805306368 | bytes 40000000 | tf_op jit(solution)/shard_map/reduce_7/pallas_call | solution.py:201
  416.7 25.6 %all-reduce.11.cloned.1.call-done = (bf16[512,3,256]{0,2,1:T(8,128)(2,1)}, bf16[256,512]{1,0:T(8,128)(2,1)}) async-done(((bf16[512,3,256]{0,2,1:T(8,128)(2,1)}, bf16[256,512]{1,0:T(8,128)(2,1)}), (bf16[512,3,256]{0,2,1:T(8,128)(2,1)}, bf16[256,512]{1,0:T(8,128)(2,1)})) %all-reduce.11.cloned.1.call-update) | async-done | bytes 1048592 | tf_op jit(solution)/shard_map/psum | solution.py:517
  442.3 2.6 copy.92
  (271 shorter events, 107.0 us)
Async XLA Ops:
  7.2 60.0 %copy-start = (f32[2,256]{1,0:T(2,128)S(1)}, f32[2,256]{1,0:T(2,128)}, u32[]{:S(2)}) copy-start(f32[2,256]{1,0:T(2,128)} %param.17) | copy-start | bytes 6148
  7.2 101.2 %all-gather.2.cloned.1.call-start = ((), (), s32[]{:S(2)}) async-start(), calls=%async_computation | async-start | bytes 2621440 | tf_op jit(solution)/shard_map/all_gather | solution.py:437
  8.8 66.9 %collective-permute-start = (bf16[512,3,128]{0,2,1:T(8,128)(2,1)S(1)}, bf16[512,3,128]{0,2,1:T(8,128)(2,1)}, u32[]{:S(2)}, u32[]{:S(2)}) collective-permute-start(bf16[512,3,128]{0,2,1:T(8,128)(2,1)S(1)} %copy.107), channel_id=1, source_target_pairs={{0,4},{4,0},{1,5},{5,1},{2,6},{6,2},{3,7},{7,3},{8,12},{12,8},{9,1... | collective-permute-start | bytes 1179656 | tf_op jit(solution)/shard_map/ppermute | solution.py:308
  11.9 57.4 %collective-permute-start.1 = (s32[1]{0:T(128)}, s32[1]{0:T(128)}, u32[]{:S(2)}, u32[]{:S(2)}) collective-permute-start(s32[1]{0:T(128)} %param.28), channel_id=1, source_target_pairs={{0,4},{4,0},{1,5},{5,1},{2,6},{6,2},{3,7},{7,3},{8,12},{12,8},{9,1... | collective-permute-start | bytes 20 | tf_op jit(solution)/shard_map/ppermute | solution.py:318
  13.3 58.7 %collective-permute-start.2 = (f32[6,512]{1,0:T(8,128)}, f32[6,512]{1,0:T(8,128)}, u32[]{:S(2)}, u32[]{:S(2)}) collective-permute-start(f32[6,512]{1,0:T(8,128)} %stack.45), channel_id=1, source_target_pairs={{0,4},{4,0},{1,5},{5,1},{2,6},{6,2},{3,7},{7,3},{8,12},{12,8},{9,1... | collective-permute-start | bytes 36872 | tf_op jit(solution)/shard_map/ppermute | solution.py:318
  27.1 307.0 %all-reduce.7.cloned.1.call-start = ((), (), s32[]{:S(2)}) async-start(), calls=%async_computation.1 | async-start | bytes 2097152 | tf_op jit(solution)/shard_map/psum | solution.py:475
  28.0 40.5 %copy-start.42 = (bf16[256,512]{1,0:T(8,128)(2,1)S(1)}, bf16[256,512]{1,0:T(8,128)(2,1)}, u32[]{:S(2)}) copy-start(bf16[256,512]{1,0:T(8,128)(2,1)} %param.29) | copy-start | bytes 786436
  28.0 40.6 %copy-start.65 = (f32[1024]{0:T(1024)S(1)}, f32[1024]{0:T(1024)}, u32[]{:S(2)}) copy-start(f32[1024]{0:T(1024)} %param.23) | copy-start | bytes 12292
  28.0 77.1 %collective-permute-start.3 = (bf16[512,512]{1,0:T(8,128)(2,1)}, bf16[512,512]{1,0:T(8,128)(2,1)}, u32[]{:S(2)}, u32[]{:S(2)}) collective-permute-start(bf16[512,512]{1,0:T(8,128)(2,1)} %constant_dynamic-slice_fusion.9), channel_id=1, source_target_pairs={{0,4},{4,0},{1,5},{5,1},{2,6},{6,2},{3,7},{7,3},{8,12},{12,8},{9,1... | collective-permute-start | bytes 1572872 | tf_op jit(solution)/shard_map/ppermute | solution.py:308
  30.6 71.8 %collective-permute-start.4 = (bf16[512,512]{1,0:T(8,128)(2,1)}, bf16[512,512]{1,0:T(8,128)(2,1)}, u32[]{:S(2)}, u32[]{:S(2)}) collective-permute-start(bf16[512,512]{1,0:T(8,128)(2,1)} %constant_dynamic-slice_fusion.8), channel_id=1, source_target_pairs={{0,4},{4,0},{1,5},{5,1},{2,6},{6,2},{3,7},{7,3},{8,12},{12,8},{9,1... | collective-permute-start | bytes 1572872 | tf_op jit(solution)/shard_map/ppermute | solution.py:308
  69.2 5.8 %collective-permute-start.6 = (bf16[128,512]{1,0:T(8,128)(2,1)S(1)}, bf16[128,512]{1,0:T(8,128)(2,1)S(1)}, u32[]{:S(2)}, u32[]{:S(2)}) collective-permute-start(bf16[128,512]{1,0:T(8,128)(2,1)S(1)} %constant_dynamic-slice_fusion.6), channel_id=1, source_target_pairs={{0,4},{4,0},{1,5},{5,1},{2,6},{6,2},{3,7},{7,3},{8,12},{12,8},{9,1... | collective-permute-start | bytes 393224 | tf_op jit(solution)/shard_map/ppermute | solution.py:308
  249.2 93.8 %collective-permute-start.9 = (bf16[128,512]{1,0:T(8,128)(2,1)}, bf16[128,512]{1,0:T(8,128)(2,1)}, u32[]{:S(2)}, u32[]{:S(2)}) collective-permute-start(bf16[128,512]{1,0:T(8,128)(2,1)} %constant_dynamic-slice_fusion.3), channel_id=1, source_target_pairs={{0,4},{4,0},{1,5},{5,1},{2,6},{6,2},{3,7},{7,3},{8,12},{12,8},{9,1... | collective-permute-start | bytes 393224 | tf_op jit(solution)/shard_map/ppermute | solution.py:308
  251.2 15.9 %collective-permute-start.11 = (bf16[512,512]{1,0:T(8,128)(2,1)}, bf16[512,512]{1,0:T(8,128)(2,1)}, u32[]{:S(2)}, u32[]{:S(2)}) collective-permute-start(bf16[512,512]{1,0:T(8,128)(2,1)} %constant_dynamic-slice_fusion.1), channel_id=1, source_target_pairs={{0,4},{4,0},{1,5},{5,1},{2,6},{6,2},{3,7},{7,3},{8,12},{12,8},{9,1... | collective-permute-start | bytes 1572872 | tf_op jit(solution)/shard_map/ppermute | solution.py:308
  252.8 25.5 %collective-permute-start.10 = (bf16[512,512]{1,0:T(8,128)(2,1)}, bf16[512,512]{1,0:T(8,128)(2,1)}, u32[]{:S(2)}, u32[]{:S(2)}) collective-permute-start(bf16[512,512]{1,0:T(8,128)(2,1)} %constant_dynamic-slice_fusion.2), channel_id=1, source_target_pairs={{0,4},{4,0},{1,5},{5,1},{2,6},{6,2},{3,7},{7,3},{8,12},{12,8},{9,1... | collective-permute-start | bytes 1572872 | tf_op jit(solution)/shard_map/ppermute | solution.py:308
  254.7 88.3 %collective-permute-start.5 = (bf16[128,512]{1,0:T(8,128)(2,1)}, bf16[128,512]{1,0:T(8,128)(2,1)}, u32[]{:S(2)}, u32[]{:S(2)}) collective-permute-start(bf16[128,512]{1,0:T(8,128)(2,1)} %constant_dynamic-slice_fusion.7), channel_id=1, source_target_pairs={{0,4},{4,0},{1,5},{5,1},{2,6},{6,2},{3,7},{7,3},{8,12},{12,8},{9,1... | collective-permute-start | bytes 393224 | tf_op jit(solution)/shard_map/ppermute | solution.py:308
  261.4 149.1 %collective-permute-start.7 = (f32[128,512]{1,0:T(8,128)}, f32[128,512]{1,0:T(8,128)}, u32[]{:S(2)}, u32[]{:S(2)}) collective-permute-start(f32[128,512]{1,0:T(8,128)} %constant_dynamic-slice_fusion.5), channel_id=1, source_target_pairs={{0,4},{4,0},{1,5},{5,1},{2,6},{6,2},{3,7},{7,3},{8,12},{12,8},{9,1... | collective-permute-start | bytes 786440 | tf_op jit(solution)/shard_map/ppermute | solution.py:308
  281.8 106.4 %all-reduce.9.cloned.1.call-start = ((), (), s32[]{:S(2)}) async-start(), calls=%async_computation.2 | async-start | bytes 2097152 | tf_op jit(solution)/shard_map/psum | solution.py:489
  285.6 59.2 %collective-permute-start.8 = (bf16[512,3,128]{0,2,1:T(8,128)(2,1)}, bf16[512,3,128]{0,2,1:T(8,128)(2,1)S(1)}, u32[]{:S(2)}, u32[]{:S(2)}) collective-permute-start(bf16[512,3,128]{0,2,1:T(8,128)(2,1)} %constant_dynamic-slice_fusion.4), channel_id=1, source_target_pairs={{0,4},{4,0},{1,5},{5,1},{2,6},{6,2},{3,7},{7,3},{8,12},{12,8},{9,1... | collective-permute-start | bytes 1179656 | tf_op jit(solution)/shard_map/ppermute | solution.py:308
  290.4 52.6 %copy-start.31 = (bf16[128,1024]{1,0:T(8,128)(2,1)S(1)}, bf16[128,1024]{1,0:T(8,128)(2,1)}, u32[]{:S(2)}) copy-start(bf16[128,1024]{1,0:T(8,128)(2,1)} %get-tuple-element.94) | copy-start | bytes 786436
  290.4 52.6 %copy-start.33 = (bf16[128,1024]{1,0:T(8,128)(2,1)S(1)}, bf16[128,1024]{1,0:T(8,128)(2,1)}, u32[]{:S(2)}) copy-start(bf16[128,1024]{1,0:T(8,128)(2,1)} %convolution_convert_fusion.3) | copy-start | bytes 786436
  299.1 35.3 %copy-start.23 = (f32[64,1024]{1,0:T(8,128)S(1)}, f32[64,1024]{1,0:T(8,128)}, u32[]{:S(2)}) copy-start(f32[64,1024]{1,0:T(8,128)} %gather_8.1) | copy-start | bytes 786436
  302.4 42.5 %copy-start.12 = (bf16[384,1024]{1,0:T(8,128)(2,1)S(1)}, bf16[384,1024]{1,0:T(8,128)(2,1)}, u32[]{:S(2)}) copy-start(bf16[384,1024]{1,0:T(8,128)(2,1)} %copy-done.11) | copy-start | bytes 2359300
  334.1 108.2 %all-reduce.11.cloned.1.call-start = ((), (), s32[]{:S(2)}) async-start(), calls=%async_computation.3 | async-start | bytes 2097152 | tf_op jit(solution)/shard_map/psum | solution.py:517
  415.2 30.6 %copy-start.1 = (f32[2,256]{1,0:T(2,128)S(1)}, f32[2,256]{1,0:T(2,128)}, u32[]{:S(2)}) copy-start(f32[2,256]{1,0:T(2,128)} %param.17) | copy-start | bytes 6148
  (59 other events, 408.6 us)
Sparse Core Ops, SparseCore 0:
  27.2 28.1 all-gather.1
  281.9 52.1 all-reduce.6
  337.0 51.1 all-reduce.8
  391.1 51.1 all-reduce.10
